TPU v7x, 256 devices: a whole 4x4x8 slice. The times are simulated.
256 devices in a mesh: dp: 16 (over z, x_hi), tensor: 16 (over x_lo, y, core).
Axes of the slice: x: 4 (x_hi: 2, x_lo: 2; x = x_hi * 2 + x_lo), y: 4, z: 8, core: 2. Of those that a mesh axis runs over, the one named last changes fastest.
Arguments:
- inputs: bfloat16 [8192, 2304], P(('dp', 'tensor')), may hold values from -6 to 6
- out_grad: bfloat16 [8192, 2304], P(('dp', 'tensor')), may hold values from -0.59765625 to 0.59765625
- gate_pre: bfloat16 [8192, 18432], P('dp', 'tensor'), may hold values from -6 to 6
- up_pre: bfloat16 [8192, 18432], P('dp', 'tensor'), may hold values from -6 to 6
- w_down: bfloat16 [18432, 2304], P('tensor'), may hold values from -0.046875 to 0.046875
- proj_new: bfloat16 [2304, 3, 256], replicated, may hold values from -0.125 to 0.125
- proj_old: bfloat16 [2304, 3, 256], P('tensor'), may hold values from -0.125 to 0.125
- first_old: float32 [256, 3, 18432], P('dp', None, 'tensor'), may hold values from -6 to 6
- second_old: float32 [256, 3, 18432], P('dp', None, 'tensor'), may hold values from 0.1 to 10
Outputs:
- first_new: float32 [256, 3, 18432], P('dp', None, 'tensor')
- second_new: float32 [256, 3, 18432], P('dp', None, 'tensor')
All inputs are finite; a program needn't handle non-finite values.
Results may differ from a plain program's by a relative error of at most 0.0005.
Values may be sent and summed in bfloat16 or wider, within the bound.
A program may use at most 64 MiB of HBM per device.

v0:
```python
import jax
import jax.numpy as jnp
from jax import lax
from jax.sharding import PartitionSpec as P

coeff = 0.7978845608028654


def gelu_pair(gate):
    inner = coeff * (gate + 0.044715 * gate * gate * gate)
    tval = jnp.tanh(inner)
    value = 0.5 * gate * (1.0 + tval)
    slope = 0.5 * (1.0 + tval) + 0.5 * gate * (1.0 - tval * tval) * coeff * (
        1.0 + 3.0 * 0.044715 * gate * gate
    )
    return (value, slope)


def on_device(
    inputs, out_grad, gate_pre, up_pre, w_down, proj_new, proj_old, first_old, second_old
):
    width = proj_new.shape[0]
    rank = proj_new.shape[2]
    flat = proj_new.reshape(width, 3 * rank)
    in_side = flat[:, : 2 * rank]
    out_side = flat[:, 2 * rank :]
    slab = width // lax.axis_size("tensor")
    own_new = lax.dynamic_slice_in_dim(proj_new, lax.axis_index("tensor") * slab, slab, 0)
    partial_rot = jnp.einsum("dki,dkj->kij", own_new, proj_old, preferred_element_type=jnp.float32)
    rotation = lax.psum(partial_rot, "tensor")
    in_proj = jnp.dot(
        lax.all_gather(inputs, "tensor", axis=0, tiled=True),
        in_side,
        preferred_element_type=jnp.float32,
    ).astype(jnp.bfloat16)
    piece = lax.all_gather(out_grad, "tensor", axis=0, tiled=True)
    hidden_rows = lax.dot_general(
        piece, w_down, (((1,), (1,)), ((), ())), preferred_element_type=jnp.float32
    )
    out_rows = jnp.dot(piece, out_side, preferred_element_type=jnp.float32).astype(jnp.bfloat16)
    value, slope = gelu_pair(gate_pre.astype(jnp.float32))
    up_rows = up_pre.astype(jnp.float32)
    gate_grad = (hidden_rows * up_rows * slope).astype(jnp.bfloat16)
    up_grad = (hidden_rows * value).astype(jnp.bfloat16)
    hidden = (value * up_rows).astype(jnp.bfloat16)
    contract = (((0,), (0,)), ((), ()))
    low_gate = lax.dot_general(
        in_proj[:, :rank], gate_grad, contract, preferred_element_type=jnp.float32
    )
    low_up = lax.dot_general(
        in_proj[:, rank:], up_grad, contract, preferred_element_type=jnp.float32
    )
    low_down = lax.dot_general(out_rows, hidden, contract, preferred_element_type=jnp.float32)
    low_grad = jnp.stack([low_gate, low_up, low_down], axis=1)
    full_first, full_second = (
        lax.all_gather(first_old, "dp", axis=0, tiled=True),
        lax.all_gather(second_old, "dp", axis=0, tiled=True),
    )
    summed = lax.psum_scatter(low_grad, "dp", scatter_dimension=0, tiled=True)
    share = first_old.shape[0]
    rot_rows = lax.dynamic_slice_in_dim(rotation, lax.axis_index("dp") * share, share, 1)
    turned_first = jnp.einsum("kij,jkc->ikc", rot_rows, full_first, precision=lax.Precision.HIGHEST)
    turned_second = jnp.einsum(
        "kij,jkc->ikc", rot_rows * rot_rows, full_second, precision=lax.Precision.HIGHEST
    )
    first_new = 0.9 * turned_first + 0.1 * summed
    second_new = 0.999 * turned_second + 0.001 * summed * summed
    return (first_new, second_new)


def solution(mesh):
    placed = (
        P(("dp", "tensor"), None),
        P(("dp", "tensor"), None),
        P("dp", "tensor"),
        P("dp", "tensor"),
        P("tensor", None),
        P(),
        P("tensor", None, None),
        P("dp", None, "tensor"),
        P("dp", None, "tensor"),
    )
    return jax.shard_map(
        on_device,
        mesh=mesh,
        in_specs=placed,
        out_specs=(P("dp", None, "tensor"), P("dp", None, "tensor")),
        check_vma=False,
    )
```

profile of v0, /device:TPU:6, one launch (start us, length us, event | category | flops | bytes accessed | tf_op | source)
XLA Modules:
  0.0 634.0 jit_solution(3412581405455012115)
XLA Ops:
  7.2 0.7 all-gather.7.cloned.1.call-update
  8.0 0.7 all-gather.9.cloned.1.call-update
  8.7 0.0 all-reduce.2.cloned.1.call-start
  8.7 2.2 fusion.27
  11.0 0.0 all-gather.11.cloned.1.call-start
  11.0 0.5 all-gather.11.cloned.1.call-update
  11.6 5.8 copy.11
  17.4 31.5 %all-gather.7.cloned.1.call-done = bf16[512,2304]{1,0:T(8,128)(2,1)} async-done(((bf16[32,2304]{1,0:T(8,128)(2,1)}), bf16[512,2304]{1,0:T(8,128)(2,1)}) %all-gather.7.cloned.1.call-update) | async-done | bytes 2359312 | tf_op jit(solution)/shard_map/all_gather | solution.py:32
  49.0 3.8 fusion.17
  52.8 34.8 %all-gather.9.cloned.1.call-done = bf16[512,2304]{1,0:T(8,128)(2,1)} async-done(((bf16[32,2304]{1,0:T(8,128)(2,1)}), bf16[512,2304]{1,0:T(8,128)(2,1)}) %all-gather.9.cloned.1.call-update) | async-done | bytes 2359312 | tf_op jit(solution)/shard_map/all_gather | solution.py:36
  87.6 6.5 %fusion.48 = f32[512,1152]{1,0:T(8,128)S(1)} fusion(bf16[512,2304]{1,0:T(8,128)(2,1)} %all-gather.9.cloned.1.call-done, bf16[1152,2304]{1,0:T(8,128)(2,1)} %param.13), kind=kOutput, calls=%fused_computation.60 | convolution fusion | flops 2717908992 | bytes 10027008 | tf_op jit(solution)/shard_map/dot_general | solution.py:37
  94.1 1.4 copy-done.3
  95.5 1.2 convolution_bitcast_fusion.1
  96.7 4.8 convolution_bitcast_fusion
  101.5 4.3 convolution_bitcast_fusion.2
  105.9 2.1 pad_maximum_fusion
  108.0 0.2 all-gather.5.cloned.1.call-start
  108.2 0.3 all-gather.5.cloned.1.call-update
  108.6 106.4 %all-reduce.2.cloned.1.call-done = f32[3,256,256]{2,1,0:T(8,128)} async-done(((f32[3,256,256]{2,1,0:T(8,128)}), f32[3,256,256]{2,1,0:T(8,128)}) %all-reduce.2.cloned.1.call-update) | async-done | bytes 786448 | tf_op jit(solution)/shard_map/psum | solution.py:30
  215.0 97.8 %all-gather.11.cloned.1.call-done = f32[256,3,1152]{2,0,1:T(8,128)} async-done(((f32[16,3,1152]{2,0,1:T(8,128)}), f32[256,3,1152]{2,0,1:T(8,128)}) %all-gather.11.cloned.1.call-update) | async-done | bytes 3538960 | tf_op jit(solution)/shard_map/all_gather | solution.py:57
  312.8 213.9 %reduce-scatter.2.cloned.1.call-done = f32[16,3,1152]{2,0,1:T(8,128)} async-done(((f32[256,3,1152]{2,0,1:T(8,128)}), f32[16,3,1152]{2,0,1:T(8,128)}) %reduce-scatter.2.cloned.1.call-update) | async-done | bytes 221200 | tf_op jit(solution)/shard_map/reduce_scatter | solution.py:59
  526.8 4.5 fusion.16
  531.3 91.4 %all-gather.5.cloned.1.call-done = f32[256,3,1152]{2,0,1:T(8,128)} async-done(((f32[16,3,1152]{2,0,1:T(8,128)}), f32[256,3,1152]{2,0,1:T(8,128)}) %all-gather.5.cloned.1.call-update) | async-done | bytes 3538960 | tf_op jit(solution)/shard_map/all_gather | solution.py:56
  622.7 4.5 fusion.14
  (12 shorter events, 0.2 us)
Async XLA Ops:
  7.2 1.6 copy-start
  7.2 41.8 %all-gather.7.cloned.1.call-start = ((), (), s32[]{:S(2)}) async-start(), calls=%async_computation.3 | async-start | bytes 2506752 | tf_op jit(solution)/shard_map/all_gather | solution.py:32
  7.9 79.7 %all-gather.9.cloned.1.call-start = ((), (), s32[]{:S(2)}) async-start(), calls=%async_computation.4 | async-start | bytes 2506752 | tf_op jit(solution)/shard_map/all_gather | solution.py:36
  8.7 206.3 %all-reduce.2.cloned.1.call-start = ((), (), s32[]{:S(2)}) async-start(), calls=%async_computation.1 | async-start | bytes 1572864 | tf_op jit(solution)/shard_map/psum | solution.py:30
  11.0 301.9 %all-gather.11.cloned.1.call-start = ((), (), s32[]{:S(2)}) async-start(), calls=%async_computation.6 | async-start | bytes 3760128 | tf_op jit(solution)/shard_map/all_gather | solution.py:57
  11.5 515.2 %reduce-scatter.2.cloned.1.call-start = ((), (), s32[]{:S(2)}) async-start(), calls=%async_computation.5 | async-start | bytes 3760128 | tf_op jit(solution)/shard_map/reduce_scatter | solution.py:59
  52.8 42.7 %copy-start.2 = (bf16[512,1152]{1,0:T(8,128)(2,1)S(1)}, bf16[512,1152]{1,0:T(8,128)(2,1)}, u32[]{:S(2)}) copy-start(bf16[512,1152]{1,0:T(8,128)(2,1)} %param.11) | copy-start | bytes 3538948
  94.1 1.4 copy-start.3
  108.0 514.7 %all-gather.5.cloned.1.call-start = ((), (), s32[]{:S(2)}) async-start(), calls=%async_computation.2 | async-start | bytes 3760128 | tf_op jit(solution)/shard_map/all_gather | solution.py:56
  526.8 95.9 %copy-start.1 = (f32[16,3,1152]{2,0,1:T(8,128)S(1)}, f32[16,3,1152]{2,0,1:T(8,128)}, u32[]{:S(2)}) copy-start(f32[16,3,1152]{2,0,1:T(8,128)} %reduce-scatter.2.cloned.1.call-done) | copy-start | bytes 663556
Sparse Core Ops, SparseCore 0:
  9.8 39.1 all-gather.6
  50.8 36.7 all-gather.8
  90.2 124.7 all-reduce.1
  217.5 95.3 all-gather.10
  316.7 210.0 reduce-scatter.1
  529.2 93.4 all-gather.4
where the time goes:
time: 636 us; the launch traced here: 634 us
  waiting for transfers between devices  578 us (91%)
  matrix products  31.9 us (5%)
  between operations  14.2 us (2%)
  local copies, waits for them, and re-layouts  7.26 us (1%)
    reduce_scatter x1, waiting for transfers between devices, on_device(): summed = lax.psum_scatter(low_grad, 'dp', scatter_dimension=0, tiled=True)  214 us
    psum x1, waiting for transfers between devices, on_device(): rotation = lax.psum(partial_rot, 'tensor')  106 us
    all_gather x1, waiting for transfers between devices, on_device(): lax.all_gather(second_old, 'dp', axis=0, tiled=True)  97.8 us
    all_gather x1, waiting for transfers between devices, on_device(): lax.all_gather(first_old, 'dp', axis=0, tiled=True)  91.4 us
    all_gather x1, waiting for transfers between devices, on_device(): piece = lax.all_gather(out_grad, 'tensor', axis=0, tiled=True)  34.8 us
    all_gather x1, waiting for transfers between devices, on_device(): lax.all_gather(inputs, 'tensor', axis=0, tiled=True)  31.5 us
  transfers between devices with their start and end apart: 6, of which 6 were waited for; matrix products, arithmetic and copies ran while one was open for 6% of the time, Pallas kernels for 0%

commit v1 on v0

v1 whole, which is shorter than its diff:
```python
import jax
import jax.numpy as jnp
from jax import lax
from jax.experimental import pallas as pl
from jax.experimental.pallas import tpu as pltpu
from jax.sharding import PartitionSpec as P

coeff = 0.7978845608028654
F32 = jnp.float32
BF16 = jnp.bfloat16
D = 2304
C = 1152
TOK = 512
SH = 32
RANK = 256
SLAB = 144
CH = 384
QT0 = (0, 9, 15, 21)
QN = (9, 6, 6, 6)
TOP = 32768.0
MESH = pl.DeviceIdType.MESH


def enc(x, buf):
    n, rows, _ = x.shape
    top = jnp.max(jnp.max(jnp.abs(x), axis=0, keepdims=True), axis=1, keepdims=True)
    top = jnp.broadcast_to(jnp.maximum(top, 1e-30), (1, rows, 128)).astype(BF16)
    buf[pl.ds(n, 1)] = top
    u = x * (TOP / top.astype(F32))
    u2 = u * u
    u4 = u2 * u2
    buf[pl.ds(0, n)] = ((u4 * u2) * (u * jnp.abs(u))).astype(BF16)


def dec(buf, n):
    v = buf[pl.ds(0, n)].astype(F32)
    r = jnp.exp2(jnp.log2(jnp.abs(v)) * 0.125)
    scale = buf[pl.ds(n, 1)].astype(F32) * (1.0 / TOP)
    return jnp.where(v < 0.0, -r, r) * scale


def kernel(
    inp_h, og_h, gate_h, up_h, w_h, pn_h, po_h, fo_h, so_h,
    of_ref, os_ref,
    inp, Y, Pb, old, gate, up, w, pn, V, U, G, H, GG, UG, L, R, M, T, TB, FIN, LOW,
    lsend, lrecv, ssend, srecv, xsend, xrecv,
    ld, gs, gr, ms, mr, ts, tr, ls, lr, ss, sr, xs, xr,
):
    d = lax.axis_index("dp")
    t = lax.axis_index("tensor")
    z = d // 2
    xh = lax.rem(d, 2)
    c = lax.rem(t, 2)
    y = lax.rem(t // 2, 4)
    xl = t // 8
    kd = jnp.minimum(d // 5, 2)

    def tid(a, b):
        return a * 8 + b * 2 + c

    yn = lax.rem(y + 1, 4)
    yb = lax.rem(y + 3, 4)
    y2 = lax.rem(y + 2, 4)
    xo = 1 - xl
    sib = t + 1 - 2 * c
    xp = tid(xo, y)
    yp = tid(xl, yn)
    ym = tid(xl, yb)
    zn = lax.rem(z + 1, 8)
    zb = lax.rem(z + 7, 8)
    zlong = jnp.where(c == 0, zn, zb)
    zshort = jnp.where(c == 0, zb, zn)
    dlong = zlong * 2 + xh
    dshort = zshort * 2 + xh
    dx = d + 1 - 2 * xh
    step = 1 - 2 * c

    def loc(src, dst, i):
        return pltpu.make_async_copy(src, dst, ld.at[i])

    own = pl.ds(pl.multiple_of(t * SH, SH), SH)
    loads = [
        loc(og_h, Y.at[own], 0),
        loc(inp_h, inp, 1),
        loc(pn_h, pn, 2),
        loc(po_h.at[kd], old.at[pl.ds(pl.multiple_of(t * SLAB, 16), SLAB)], 3),
        loc(gate_h, gate, 4),
        loc(up_h, up, 5),
        loc(w_h, w, 6),
    ]
    for a in loads:
        a.start()

    bar = pltpu.get_barrier_semaphore()
    for peer in (sib, xp, yp, ym):
        pl.semaphore_signal(bar, inc=1, device_id={"tensor": peer}, device_id_type=MESH)

    @pl.loop(1, 16)
    def _(j):
        pl.semaphore_signal(
            bar, inc=1, device_id={"dp": lax.rem(d + j, 16)}, device_id_type=MESH
        )

    for a in loads[:3]:
        a.wait()
    for k in range(3):
        lhs = inp[...] if k < 2 else Y[own, :]
        Pb[own, k * RANK : (k + 1) * RANK] = jnp.dot(
            lhs, pn[k], preferred_element_type=F32
        ).astype(BF16)
    loads[3].wait()
    pl.semaphore_wait(bar, 19)

    pay = ((Pb, SH, SH), (Y, SH, SH), (old, SLAB, 16))

    def gcopy(p, slot, target, i):
        buf, rows, mult = pay[p]
        sl = pl.ds(pl.multiple_of(slot * rows, mult), rows)
        return pltpu.make_async_remote_copy(
            src_ref=buf.at[sl], dst_ref=buf.at[sl], send_sem=gs.at[p, i],
            recv_sem=gr.at[p, slot], device_id={"tensor": target}, device_id_type=MESH,
        )

    def gsend(p, slot, target, i):
        gcopy(p, slot, target, i).start()

    def gwait(p, slot):
        gcopy(p, slot, sib, 0).wait_recv()

    def g0(p):
        gsend(p, t, xp, 0)
        gsend(p, t, yp, 1)
        gsend(p, t, ym, 2)
        gsend(p, t, sib, 3)

    dfrom = jnp.where(c == 0, ym, yp)
    dto = jnp.where(c == 0, yp, ym)

    def g1(p):
        gwait(p, xp)
        gsend(p, xp, yp, 4)
        gsend(p, xp, ym, 5)
        gsend(p, xp, sib, 6)
        gwait(p, ym)
        gwait(p, yp)
        gsend(p, dfrom, dto, 7)
        gsend(p, ym, sib, 8)
        gsend(p, yp, sib, 9)

    def g2(p):
        far = tid(xl, y2)
        gwait(p, far)
        gsend(p, far, xp, 12)
        gsend(p, far, sib, 13)
        gwait(p, tid(xo, yb))
        gsend(p, tid(xo, yb), sib, 10)
        gwait(p, tid(xo, yn))
        gsend(p, tid(xo, yn), sib, 11)
        gwait(p, tid(xo, y2))
        gsend(p, tid(xo, y2), sib, 14)

    def g3(p):
        @pl.loop(0, 8)
        def _(j):
            gwait(p, j * 2 + 1 - c)

    def colof(e):
        return pl.multiple_of(jnp.minimum(e * 256, 896), 128)

    def mrem(m, o, src):
        return pltpu.make_async_remote_copy(
            src_ref=src, dst_ref=M.at[m, pl.ds(pl.multiple_of(d * 16, 16), 16)],
            send_sem=ms.at[m, o], recv_sem=mr.at[m, d],
            device_id={"dp": o}, device_id_type=MESH,
        )

    def msend():
        @pl.loop(0, 15)
        def _(o):
            for m, ref in enumerate((fo_h, so_h)):
                src = ref.at[o // 5, :, pl.ds(colof(lax.rem(o, 5)), 256)]

                @pl.when(o != d)
                def _():
                    mrem(m, o, src).start()

                @pl.when(o == d)
                def _():
                    pltpu.make_async_copy(
                        src, M.at[m, pl.ds(pl.multiple_of(d * 16, 16), 16)], mr.at[m, d]
                    ).start()

    def trem(m, dst, o):
        return pltpu.make_async_remote_copy(
            src_ref=T.at[m, pl.ds(pl.multiple_of(dst * 16, 16), 16)], dst_ref=TB.at[m, o],
            send_sem=ts.at[m, dst], recv_sem=tr.at[m, o],
            device_id={"dp": dst}, device_id_type=MESH,
        )

    def turn():
        R[...] = lax.dot_general(
            pn[kd], old[...], (((0,), (0,)), ((), ())), preferred_element_type=F32
        )

        @pl.when(d < 15)
        def _():
            @pl.loop(0, 16)
            def _(s):
                for m in range(2):
                    pltpu.make_async_copy(
                        M.at[m, pl.ds(pl.multiple_of(s * 16, 16), 16)],
                        M.at[m, pl.ds(pl.multiple_of(s * 16, 16), 16)], mr.at[m, s]
                    ).wait()

            rot = R[...]
            for m in range(2):
                T[m] = jnp.dot(
                    rot if m == 0 else rot * rot, M[m],
                    precision=lax.Precision.HIGHEST, preferred_element_type=F32,
                )

            @pl.loop(0, 16)
            def _(j):
                for m in range(2):
                    @pl.when(j != d)
                    def _():
                        trem(m, j, d).start()

                    @pl.when(j == d)
                    def _():
                        pltpu.make_async_copy(
                            T.at[m, pl.ds(pl.multiple_of(d * 16, 16), 16)], TB.at[m, d],
                            tr.at[m, d],
                        ).start()

    def lcopy(q, r):
        n = QN[q] + 1
        t0 = QT0[q] + q
        return pltpu.make_async_remote_copy(
            src_ref=lsend.at[r, pl.ds(t0, n)], dst_ref=lrecv.at[r, pl.ds(t0, n)],
            send_sem=ls.at[q, r], recv_sem=lr.at[q, r],
            device_id={"dp": dlong}, device_id_type=MESH,
        )

    def scopy(q, r):
        n = QN[q] + 1
        t0 = QT0[q] + q
        return pltpu.make_async_remote_copy(
            src_ref=ssend.at[r, pl.ds(t0, n)], dst_ref=srecv.at[r, pl.ds(t0, n)],
            send_sem=ss.at[q, r], recv_sem=sr.at[q, r],
            device_id={"dp": dshort}, device_id_type=MESH,
        )

    def mine(q, zdest):
        return L[pl.ds(QT0[q], QN[q]), pl.ds(pl.multiple_of(zdest * 32, 32), 32), :]

    def rnd(q, r):
        n = QN[q]
        tiles = pl.ds(QT0[q] + q, n + 1)
        x = mine(q, lax.rem(z + 8 + step * (4 - r), 8))
        if r > 0:
            lcopy(q, r - 1).wait_recv()
            x = x + dec(lrecv.at[r - 1, tiles], n)
        enc(x, lsend.at[r, tiles])
        lcopy(q, r).start()
        if r < 3:
            x = mine(q, lax.rem(z + 8 - step * (3 - r), 8))
            if r > 0:
                scopy(q, r - 1).wait_recv()
                x = x + dec(srecv.at[r - 1, tiles], n)
            enc(x, ssend.at[r, tiles])
            scopy(q, r).start()

    def xcopy(q):
        n = QN[q] + 1
        t0 = QT0[q] + q
        return pltpu.make_async_remote_copy(
            src_ref=xsend.at[pl.ds(t0, n)], dst_ref=xrecv.at[pl.ds(t0, n)],
            send_sem=xs.at[q], recv_sem=xr.at[q],
            device_id={"dp": dx}, device_id_type=MESH,
        )

    def fin(q):
        n = QN[q]
        tiles = pl.ds(QT0[q] + q, n + 1)
        dst = pl.ds(QT0[q], n)
        lcopy(q, 3).wait_recv()
        scopy(q, 2).wait_recv()
        FIN[dst] = mine(q, z) + dec(lrecv.at[3, tiles], n) + dec(srecv.at[2, tiles], n)
        enc(FIN[dst, pl.ds(pl.multiple_of((1 - xh) * 16, 16), 16), :], xsend.at[tiles])
        xcopy(q).start()

    def last(q):
        n = QN[q]
        tiles = pl.ds(QT0[q] + q, n + 1)
        dst = pl.ds(QT0[q], n)
        xcopy(q).wait_recv()
        LOW[dst] = FIN[dst, pl.ds(pl.multiple_of(xh * 16, 16), 16), :] + dec(xrecv.at[tiles], n)

    g0(0)
    g0(1)
    g1(0)
    g1(1)
    msend()
    g0(2)
    loads[4].wait()
    loads[5].wait()

    def act(lo, hi):
        @pl.loop(lo, hi)
        def _(i):
            rows = pl.ds(pl.multiple_of(i * 16, 16), 16)
            g = gate[rows, :].astype(F32)
            u = up[rows, :].astype(F32)
            g2_ = g * g
            tv = jnp.tanh(coeff * (g + 0.044715 * (g2_ * g)))
            val = 0.5 * g * (1.0 + tv)
            slope = 0.5 * (1.0 + tv) + 0.5 * g * (1.0 - tv * tv) * (
                coeff * (1.0 + 3.0 * 0.044715 * g2_)
            )
            V[rows, :] = val
            U[rows, :] = u * slope
            G[rows, :] = (val * u).astype(BF16)

    act(0, 16)
    g2(0)
    g2(1)
    act(16, 32)
    g3(0)

    contract = (((0,), (0,)), ((), ()))
    for j in range(3):
        r = lax.dot_general(
            Pb[:, 2 * RANK : 3 * RANK], G[:, j * CH : (j + 1) * CH], contract,
            preferred_element_type=F32,
        )
        for i in range(3):
            L[3 * j + i] = r[:, i * 128 : (i + 1) * 128]
    rnd(0, 0)
    g1(2)
    g3(1)
    loads[6].wait()

    def chunk(j):
        cols = slice(j * CH, (j + 1) * CH)
        H[...] = lax.dot_general(
            Y[...], w[cols, :], (((1,), (1,)), ((), ())), preferred_element_type=F32
        )

        @pl.loop(0, 16)
        def _(i):
            rows = pl.ds(pl.multiple_of(i * 32, 32), 32)
            h = H[rows, :]
            GG[rows, :] = (h * U[rows, cols]).astype(BF16)
            UG[rows, :] = (h * V[rows, cols]).astype(BF16)

        for k, ref in enumerate((GG, UG)):
            r = lax.dot_general(
                Pb[:, k * RANK : (k + 1) * RANK], ref[...], contract, preferred_element_type=F32
            )
            for i in range(3):
                L[9 + 6 * j + 3 * k + i] = r[:, i * 128 : (i + 1) * 128]

    chunk(0)
    rnd(0, 1)
    rnd(1, 0)
    g2(2)
    chunk(1)
    rnd(0, 2)
    rnd(1, 1)
    rnd(2, 0)
    chunk(2)
    rnd(0, 3)
    rnd(1, 2)
    rnd(2, 1)
    rnd(3, 0)
    g3(2)
    turn()
    fin(0)
    rnd(1, 3)
    rnd(2, 2)
    rnd(3, 1)
    last(0)
    fin(1)
    rnd(2, 3)
    rnd(3, 2)
    last(1)
    fin(2)
    rnd(3, 3)
    last(2)

    @pl.loop(0, 15)
    def _(o):
        for m in range(2):
            pltpu.make_async_copy(TB.at[m, o], TB.at[m, o], tr.at[m, o]).wait()

    def out(q):
        for i in range(QN[q]):
            if q == 0:
                k, ct = 2, i
            else:
                k, ct = i // 3, (q - 1) * 3 + i % 3
            e, off = (4, 128) if ct == 8 else (ct // 2, (ct % 2) * 128)
            low = LOW[QT0[q] + i]
            tf = TB[0, 5 * k + e, :, off : off + 128]
            tsq = TB[1, 5 * k + e, :, off : off + 128]
            cols = slice(ct * 128, (ct + 1) * 128)
            of_ref[k, :, cols] = 0.9 * tf + 0.1 * low
            os_ref[k, :, cols] = 0.999 * tsq + 0.001 * low * low

    for q in range(3):
        out(q)
    fin(3)
    last(3)
    out(3)

    for p in range(3):
        for i in range(15):
            gcopy(p, t, sib, i).wait_send()

    @pl.loop(0, 15)
    def _(o):
        for m in range(2):
            @pl.when(o != d)
            def _():
                mrem(m, o, fo_h.at[0, :, pl.ds(0, 256)]).wait_send()

    @pl.when(d < 15)
    def _():
        @pl.loop(0, 16)
        def _(j):
            for m in range(2):
                @pl.when(j != d)
                def _():
                    trem(m, j, d).wait_send()

    for q in range(4):
        for r in range(4):
            lcopy(q, r).wait_send()
        for r in range(3):
            scopy(q, r).wait_send()
        xcopy(q).wait_send()


def on_device(inputs, out_grad, gate_pre, up_pre, w_down, proj_new, proj_old, first_old, second_old):
    flip = lambda a: jnp.transpose(a, (1, 0, 2))
    shape = jax.ShapeDtypeStruct((3, 16, C), F32)
    dma = pltpu.SemaphoreType.DMA
    first, second = pl.pallas_call(
        kernel,
        out_shape=(shape, shape),
        in_specs=[pl.BlockSpec(memory_space=pl.ANY)] * 9,
        out_specs=(pl.BlockSpec(memory_space=pltpu.VMEM),) * 2,
        scratch_shapes=[
            pltpu.VMEM((SH, D), BF16),
            pltpu.VMEM((TOK, D), BF16),
            pltpu.VMEM((TOK, 3 * RANK), BF16),
            pltpu.VMEM((D, RANK), BF16),
            pltpu.VMEM((TOK, C), BF16),
            pltpu.VMEM((TOK, C), BF16),
            pltpu.VMEM((C, D), BF16),
            pltpu.VMEM((3, D, RANK), BF16),
            pltpu.VMEM((TOK, C), F32),
            pltpu.VMEM((TOK, C), F32),
            pltpu.VMEM((TOK, C), BF16),
            pltpu.VMEM((TOK, CH), F32),
            pltpu.VMEM((TOK, CH), BF16),
            pltpu.VMEM((TOK, CH), BF16),
            pltpu.VMEM((27, RANK, 128), F32),
            pltpu.VMEM((RANK, RANK), F32),
            pltpu.VMEM((2, RANK, RANK), F32),
            pltpu.VMEM((2, RANK, RANK), F32),
            pltpu.VMEM((2, 15, 16, 256), F32),
            pltpu.VMEM((27, 32, 128), F32),
            pltpu.VMEM((27, 16, 128), F32),
            pltpu.VMEM((4, 31, 32, 128), BF16),
            pltpu.VMEM((4, 31, 32, 128), BF16),
            pltpu.VMEM((3, 31, 32, 128), BF16),
            pltpu.VMEM((3, 31, 32, 128), BF16),
            pltpu.VMEM((31, 16, 128), BF16),
            pltpu.VMEM((31, 16, 128), BF16),
            dma((7,)), dma((3, 15)), dma((3, 16)),
            dma((2, 16)), dma((2, 16)), dma((2, 16)), dma((2, 16)),
            dma((4, 4)), dma((4, 4)), dma((4, 3)), dma((4, 3)), dma((4,)), dma((4,)),
        ],
        compiler_params=pltpu.CompilerParams(
            collective_id=0, has_side_effects=True, vmem_limit_bytes=63 * 1024 * 1024
        ),
    )(
        inputs, out_grad, gate_pre, up_pre, w_down, flip(proj_new), flip(proj_old),
        flip(first_old), flip(second_old),
    )
    return flip(first), flip(second)


def solution(mesh):
    placed = (
        P(("dp", "tensor"), None),
        P(("dp", "tensor"), None),
        P("dp", "tensor"),
        P("dp", "tensor"),
        P("tensor", None),
        P(),
        P("tensor", None, None),
        P("dp", None, "tensor"),
        P("dp", None, "tensor"),
    )
    return jax.shard_map(
        on_device,
        mesh=mesh,
        in_specs=placed,
        out_specs=(P("dp", None, "tensor"), P("dp", None, "tensor")),
        check_vma=False,
    )
```

time: 636 us -> 85.2 us (0.13)
  waiting for transfers between devices: 578 us -> 0 us
  Pallas kernels: 0 us -> 80.8 us
  matrix products: 31.9 us -> 0 us
  between operations: 14.2 us -> 0.64 us
    all_gather x4 -> x0, waiting for transfers between devices: 256 us -> none  [the longest x1 97.8 us: on_device(): lax.all_gather(second_old, 'dp', axis=0, tiled=True)]
    reduce_scatter x1 -> x0, waiting for transfers between devices: 214 us -> none  [on_device(): summed = lax.psum_scatter(low_grad, 'dp', scatter_dimension=0, tiled=True)]
    psum x1 -> x0, waiting for transfers between devices: 106 us -> none  [on_device(): rotation = lax.psum(partial_rot, 'tensor')]
    pallas_call x0 -> x1, Pallas kernels: none -> 80.8 us  [on_device(): pl.pallas_call(kernel, out_shape=(shape, shape), in_specs=[pl.BlockSpec(m...]
    dot_general x8 -> x0, matrix products: 31.9 us -> none  [the longest x1 6.47 us: on_device(): lax.dot_general(piece, w_down, (((1,), (1,)), ((), ())), preferred_elemen...]
  transfers between devices with their start and end apart: 6 -> 0, of which waited for: 6 -> 0; matrix products, arithmetic and copies ran while one was open for 6% -> 0% of each run, Pallas kernels for 0% -> 0%
where the time goes in v1:
time: 85.2 us; the launch traced here: 84.7 us
  Pallas kernels  80.8 us (95%)
  local copies, waits for them, and re-layouts  3.27 us (4%)
    pallas_call x1, Pallas kernels, on_device(): pl.pallas_call(kernel, out_shape=(shape, shape), in_specs=[pl.BlockSpec(m...  80.8 us
    unnamed x2, local copies, waits for them, and re-layouts  3.27 us

profile of v1, /device:TPU:6, one launch (start us, length us, event | category | flops | bytes accessed | tf_op | source)
XLA Modules:
  0.0 84.7 jit_solution(13159138676628130010)
XLA Ops:
  0.6 80.8 %shard_map.104 = (f32[3,16,1152]{2,1,0:T(8,128)}, f32[3,16,1152]{2,1,0:T(8,128)}) custom-call(bf16[32,2304]{1,0:T(8,128)(2,1)} %inp_h.1, bf16[32,2304]{1,0:T(8,128)(2,1)} %og_h.1, bf16[512,1152]{1,0:T(8,128)(2,1)} %gate_h.1, bf16[512,1152]{1,0:T(8,128)(2,1)} %up_h.1, bf16[1152,2304]{1,0:T(8,128)(2,1)} %w_h.1, bf16[3,2304,256]{2,1,0:T(8,128)(2,1)} %bitcast.6, ...), custom_call_target="tpu_custom_call" | custom-call | tf_op jit(solution)/shard_map/pallas_call | solution.py:449
  81.4 1.6 %copy.13 = f32[16,3,1152]{2,0,1:T(8,128)} copy(f32[16,3,1152]{2,0,1:T(8,128)} %bitcast.8) | data formatting | bytes 442368
  83.1 1.6 %copy.14 = f32[16,3,1152]{2,0,1:T(8,128)} copy(f32[16,3,1152]{2,0,1:T(8,128)} %bitcast.7) | data formatting | bytes 442368

commit v2 on v1

v2 whole, which is shorter than its diff:
```python
import jax
import jax.numpy as jnp
from jax import lax
from jax.experimental import pallas as pl
from jax.experimental.pallas import tpu as pltpu
from jax.sharding import PartitionSpec as P

coeff = 0.7978845608028654
F32 = jnp.float32
BF16 = jnp.bfloat16
D = 2304
C = 1152
TOK = 512
SH = 32
RANK = 256
SLAB = 144
CH = 384
QT0 = (0, 5, 9, 15, 21)
QN = (5, 4, 6, 6, 6)
NQ = 5
ROWS = 27 * 32 + 8 * NQ
XROWS = 27 * 16 + 8 * NQ
BACK = (0, 2, 1, 3, 5, 4, 6)
TOP = 32768.0
MESH = pl.DeviceIdType.MESH


def top_of(x):
    top = jnp.max(jnp.max(jnp.abs(x), axis=0), axis=0, keepdims=True)
    return jnp.broadcast_to(jnp.maximum(top, 1e-30), (8, 128)).astype(BF16)


def code(x, top):
    n, rows, _ = x.shape
    u = x * (TOP / top.astype(F32))[0:1][None]
    u2 = u * u
    u4 = u2 * u2
    return ((u4 * u2) * (u * jnp.abs(u))).astype(BF16).reshape(n * rows, 128)


def value(v, scale, n):
    v = v.astype(F32)
    r = jnp.exp2(jnp.log2(jnp.abs(v)) * 0.125)
    return (jnp.where(v < 0.0, -r, r) * (scale * (1.0 / TOP))).reshape(n, -1, 128)


def enc(x, buf):
    n, rows, _ = x.shape
    top = top_of(x)
    buf[pl.ds(n * rows, 8)] = top
    buf[pl.ds(0, n * rows)] = code(x, top)


def dec(buf, n, rows):
    scale = buf[pl.ds(n * rows, 8)].astype(F32)[0:1]
    return value(buf[pl.ds(0, n * rows)], scale, n)


def enc2(a, b, buf):
    ta, tb = top_of(a), top_of(b)
    first = lax.broadcasted_iota(jnp.int32, (8, 128), 0) < 4
    buf[pl.ds(64, 8)] = jnp.where(first, ta.astype(F32), tb.astype(F32)).astype(BF16)
    buf[pl.ds(0, 32)] = code(a, ta)
    buf[pl.ds(32, 32)] = code(b, tb)


def dec2(buf):
    scale = buf[pl.ds(64, 8)].astype(F32)
    return value(buf[pl.ds(0, 32)], scale[0:1], 2), value(buf[pl.ds(32, 32)], scale[4:5], 2)


def kernel(
    inp_h, og_h, gate_h, up_h, w_h, pn_h, po_h, fo_h, so_h,
    low_h, tf_h, ts_h,
    inp, Y, Pb, old, gate, up, w, pn, fo, so, V, U, G, H, GG, UG, L, R, M, T, MS, MR, TS, TB, FIN, OUT,
    rsend, rrecv, xsend, xrecv,
    ld, gs, gr, ms, mr, ts, tr, rs, rr, xs, xr,
):
    d = lax.axis_index("dp")
    t = lax.axis_index("tensor")
    z = d // 2
    xh = lax.rem(d, 2)
    c = lax.rem(t, 2)
    y = lax.rem(t // 2, 4)
    xl = t // 8
    kd = jnp.minimum(d // 5, 2)

    def tid(a, b):
        return a * 8 + b * 2 + c

    yn = lax.rem(y + 1, 4)
    yb = lax.rem(y + 3, 4)
    y2 = lax.rem(y + 2, 4)
    xo = 1 - xl
    sib = t + 1 - 2 * c
    xp = tid(xo, y)
    yp = tid(xl, yn)
    ym = tid(xl, yb)
    zn = lax.rem(z + 1, 8)
    zb = lax.rem(z + 7, 8)
    zlong = jnp.where(c == 0, zn, zb)
    zshort = jnp.where(c == 0, zb, zn)
    dlong = zlong * 2 + xh
    dshort = zshort * 2 + xh
    dx = d + 1 - 2 * xh
    step = 1 - 2 * c

    def loc(src, dst, i):
        return pltpu.make_async_copy(src, dst, ld.at[i])

    own = pl.ds(pl.multiple_of(t * SH, SH), SH)
    loads = [
        loc(og_h, Y.at[own], 0),
        loc(inp_h, inp, 1),
        loc(pn_h, pn, 2),
        loc(po_h.at[kd], old.at[pl.ds(pl.multiple_of(t * SLAB, 16), SLAB)], 3),
        loc(gate_h, gate, 4),
        loc(up_h, up, 5),
        loc(w_h, w, 6),
        loc(fo_h, fo, 7),
        loc(so_h, so, 8),
    ]
    for i in (1, 0, 2, 7, 8, 3):
        loads[i].start()

    bar = pltpu.get_barrier_semaphore()
    lane = (xp, yp, ym, tid(xl, y2), tid(xo, yn), tid(xo, yb), tid(xo, y2))
    for peer in (sib,) + lane:
        pl.semaphore_signal(bar, inc=1, device_id={"tensor": peer}, device_id_type=MESH)

    @pl.loop(1, 16)
    def _(j):
        pl.semaphore_signal(
            bar, inc=1, device_id={"dp": lax.rem(d + j, 16)}, device_id_type=MESH
        )

    pay = ((Pb, SH, SH), (Y, SH, SH), (old, SLAB, 16))

    def gcopy(p, slot, target, i):
        buf, rows, mult = pay[p]
        sl = pl.ds(pl.multiple_of(slot * rows, mult), rows)
        return pltpu.make_async_remote_copy(
            src_ref=buf.at[sl], dst_ref=buf.at[sl], send_sem=gs.at[p],
            recv_sem=gr.at[p, i], device_id={"tensor": target}, device_id_type=MESH,
        )

    def gsend(p, slot, target, i):
        gcopy(p, slot, target, i).start()

    def gwait(p, j):
        gcopy(p, lane[j], sib, j).wait_recv()

    def shards(p, n, sem):
        buf, rows, _ = pay[p]
        part = buf.at[pl.ds(0, n * rows)]
        pltpu.make_async_copy(part, part, sem).wait()

    def project():
        for a in loads[:3]:
            a.wait()
        for i in (4, 5, 6):
            loads[i].start()
        for k in range(3):
            lhs = inp[...] if k < 2 else Y[own, :]
            Pb[own, k * RANK : (k + 1) * RANK] = jnp.dot(
                lhs, pn[k], preferred_element_type=F32
            ).astype(BF16)

    def gown(p, n):
        for j in range(n):
            gsend(p, t, lane[j], BACK[j])
        gsend(p, t, sib, 7)

    def gmirror(p, js):
        for j in js:
            gwait(p, j)
            gsend(p, lane[j], sib, 7)

    def gpair(p):
        gwait(p, 0)
        gsend(p, xp, yp, 5)
        gsend(p, xp, ym, 4)
        gsend(p, xp, sib, 7)

    def gfar(p):
        gwait(p, 3)
        gsend(p, lane[3], xp, 6)
        gsend(p, lane[3], sib, 7)

    def g3(p):
        shards(p, 8, gr.at[p, 7])

    def mrem(o):
        return pltpu.make_async_remote_copy(
            src_ref=MS.at[o], dst_ref=MR.at[d], send_sem=ms, recv_sem=mr,
            device_id={"dp": o}, device_id_type=MESH,
        )

    def menc():
        loads[7].wait()
        loads[8].wait()
        for o in range(15):
            c0 = min((o % 5) * 256, 896)
            pair = [
                jnp.stack([ref[o // 5, :, c0 + i * 128 : c0 + i * 128 + 128] for i in range(2)])
                for ref in (fo, so)
            ]
            enc2(*pair, MS.at[o])

    def msend(par):
        @pl.loop(0, 8)
        def _(j):
            o = 2 * j + par

            @pl.when(jnp.logical_and(o < 15, o != d))
            def _():
                mrem(o).start()

            @pl.when(jnp.logical_and(o < 15, o == d))
            def _():
                pltpu.make_async_copy(MS.at[o], MR.at[d], mr).start()

    def trem(dst):
        return pltpu.make_async_remote_copy(
            src_ref=TS.at[dst], dst_ref=TB.at[d], send_sem=ts, recv_sem=tr,
            device_id={"dp": dst}, device_id_type=MESH,
        )

    def turn():
        R[...] = lax.dot_general(
            pn[kd], old[...], (((0,), (0,)), ((), ())), preferred_element_type=F32
        )

        @pl.when(d < 15)
        def _():
            pltpu.make_async_copy(MR, MR, mr).wait()

            @pl.loop(0, 16)
            def _(s):
                rows = pl.ds(pl.multiple_of(s * 16, 16), 16)
                for m, x in enumerate(dec2(MR.at[s])):
                    M[m, rows, 0:128] = x[0]
                    M[m, rows, 128:256] = x[1]

            rot = R[...]
            for m in range(2):
                T[m] = jnp.dot(
                    rot if m == 0 else rot * rot, M[m],
                    precision=lax.Precision.HIGHEST, preferred_element_type=F32,
                )

            @pl.loop(0, 16)
            def _(j):
                rows = pl.ds(pl.multiple_of(j * 16, 16), 16)
                pair = [jnp.stack([T[m, rows, 0:128], T[m, rows, 128:256]]) for m in range(2)]
                enc2(*pair, TS.at[j])

                @pl.when(j != d)
                def _():
                    trem(j).start()

                @pl.when(j == d)
                def _():
                    pltpu.make_async_copy(TS.at[j], TB.at[d], tr).start()

    def span(q, rows=32):
        return pl.ds(QT0[q] * rows + 8 * q, QN[q] * rows + 8)

    def rcopy(q, i):
        sp = span(q)
        return pltpu.make_async_remote_copy(
            src_ref=rsend.at[i, sp], dst_ref=rrecv.at[i, sp], send_sem=rs, recv_sem=rr.at[q, i],
            device_id={"dp": dlong if i < 4 else dshort}, device_id_type=MESH,
        )

    def mine(q, zdest):
        return L[pl.ds(QT0[q], QN[q]), pl.ds(pl.multiple_of(zdest * 32, 32), 32), :]

    def rnd(q, r):
        n = QN[q]
        tiles = span(q)
        for i, far in ((r, step * (4 - r)), (4 + r, -step * (3 - r))):
            if i == 7:
                continue
            x = mine(q, lax.rem(z + 8 + far, 8))
            if r > 0:
                rcopy(q, i - 1).wait_recv()
                x = x + dec(rrecv.at[i - 1, tiles], n, 32)
            enc(x, rsend.at[i, tiles])
            rcopy(q, i).start()

    def xcopy(q):
        sp = span(q, 16)
        return pltpu.make_async_remote_copy(
            src_ref=xsend.at[sp], dst_ref=xrecv.at[sp], send_sem=xs, recv_sem=xr.at[q],
            device_id={"dp": dx}, device_id_type=MESH,
        )

    def fin(q):
        n = QN[q]
        tiles = span(q)
        dst = pl.ds(QT0[q], n)
        rcopy(q, 3).wait_recv()
        rcopy(q, 6).wait_recv()
        FIN[dst] = mine(q, z) + dec(rrecv.at[3, tiles], n, 32) + dec(rrecv.at[6, tiles], n, 32)
        enc(FIN[dst, pl.ds(pl.multiple_of((1 - xh) * 16, 16), 16), :], xsend.at[span(q, 16)])
        xcopy(q).start()

    def last(q):
        n = QN[q]
        dst = pl.ds(QT0[q], n)
        xcopy(q).wait_recv()
        low = FIN[dst, pl.ds(pl.multiple_of(xh * 16, 16), 16), :] + dec(xrecv.at[span(q, 16)], n, 16)
        for i in range(n):
            g = QT0[q] + i
            k, ct = (2, g) if g < 9 else ((g - 9) % 6 // 3, (g - 9) // 6 * 3 + (g - 9) % 3)
            OUT[k, :, ct * 128 : (ct + 1) * 128] = low[i]
        if q < 2:
            part = (2, slice(None), pl.ds(QT0[q] * 128, n * 128))
        else:
            part = (pl.ds(0, 2), slice(None), pl.ds((q - 2) * CH, CH))
        pltpu.make_async_copy(OUT.at[part], low_h.at[part], ld.at[9]).start()

    def back():
        pltpu.make_async_copy(TB, TB, tr).wait()
        for o in range(15):
            for m, x in enumerate(dec2(TB.at[o])):
                for i in range(2):
                    ct = min(2 * (o % 5), 7) + i
                    if o % 5 < 4 or i == 1:
                        OUT[3 + 3 * m + o // 5, :, ct * 128 : (ct + 1) * 128] = x[i]
        loc(OUT.at[pl.ds(3, 3)], tf_h, 9).start()
        loc(OUT.at[pl.ds(6, 3)], ts_h, 9).start()

    project()
    pl.semaphore_wait(bar, 23)
    gown(0, 7)
    gown(1, 4)
    menc()
    msend(xh)
    loads[4].wait()
    loads[5].wait()

    def act(lo, hi):
        @pl.loop(lo, hi)
        def _(i):
            rows = pl.ds(pl.multiple_of(i * 16, 16), 16)
            g = gate[rows, :].astype(F32)
            u = up[rows, :].astype(F32)
            g2_ = g * g
            tv = jnp.tanh(coeff * (g + 0.044715 * (g2_ * g)))
            val = 0.5 * g * (1.0 + tv)
            slope = 0.5 * (1.0 + tv) + 0.5 * g * (1.0 - tv * tv) * (
                coeff * (1.0 + 3.0 * 0.044715 * g2_)
            )
            V[rows, :] = val
            U[rows, :] = u * slope
            G[rows, :] = (val * u).astype(BF16)

    contract = (((0,), (0,)), ((), ()))

    def lowd():
        for j in range(3):
            r = lax.dot_general(
                Pb[:, 2 * RANK : 3 * RANK], G[:, j * CH : (j + 1) * CH], contract,
                preferred_element_type=F32,
            )
            for i in range(3):
                L[3 * j + i] = r[:, i * 128 : (i + 1) * 128]

    def chunk(j):
        cols = slice(j * CH, (j + 1) * CH)
        H[...] = lax.dot_general(
            Y[...], w[cols, :], (((1,), (1,)), ((), ())), preferred_element_type=F32
        )

        @pl.loop(0, 16)
        def _(i):
            rows = pl.ds(pl.multiple_of(i * 32, 32), 32)
            h = H[rows, :]
            GG[rows, :] = (h * U[rows, cols]).astype(BF16)
            UG[rows, :] = (h * V[rows, cols]).astype(BF16)

        for k, ref in enumerate((GG, UG)):
            r = lax.dot_general(
                Pb[:, k * RANK : (k + 1) * RANK], ref[...], contract, preferred_element_type=F32
            )
            for i in range(3):
                L[9 + 6 * j + 3 * k + i] = r[:, i * 128 : (i + 1) * 128]

    def gdrain():
        for p in range(3):
            shards(p, 15, gs.at[p])

    def mdrain():
        @pl.when(d < 15)
        def _():
            part = MS.at[pl.ds(0, 14)]
            pltpu.make_async_copy(part, part, ms).wait()
            part = TS.at[pl.ds(0, 15)]
            pltpu.make_async_copy(part, part, ts).wait()

        @pl.when(d == 15)
        def _():
            pltpu.make_async_copy(MS, MS, ms).wait()

    def rdrain():
        pltpu.make_async_copy(rsend, rsend, rs).wait()
        pltpu.make_async_copy(xsend, xsend, xs).wait()
        pltpu.make_async_copy(OUT, OUT, ld.at[9]).wait()

    act(0, 32)
    gmirror(0, range(7))
    gpair(1)
    msend(1 - xh)
    g3(0)
    lowd()
    rnd(0, 0)
    rnd(1, 0)
    gfar(1)
    loads[3].wait()
    gown(2, 4)
    gmirror(1, (1, 2))
    rnd(0, 1)
    rnd(1, 1)
    gmirror(1, (4, 5))
    gpair(2)
    gmirror(1, (6,))
    loads[6].wait()
    rnd(0, 2)
    g3(1)
    chunk(0)
    rnd(2, 0)
    rnd(1, 2)
    gfar(2)
    gmirror(2, (1, 2, 4, 5))
    rnd(0, 3)
    chunk(1)
    rnd(3, 0)
    rnd(2, 1)
    rnd(1, 3)
    gmirror(2, (6,))
    g3(2)
    turn()
    fin(0)
    rnd(3, 1)
    rnd(2, 2)
    chunk(2)
    rnd(4, 0)
    rnd(3, 2)
    rnd(2, 3)
    fin(1)
    rnd(4, 1)
    last(0)
    last(1)
    rnd(3, 3)
    fin(2)
    rnd(4, 2)
    fin(3)
    rnd(4, 3)
    last(2)
    gdrain()
    mdrain()
    back()
    fin(4)
    last(3)
    last(4)
    rdrain()


def on_device(inputs, out_grad, gate_pre, up_pre, w_down, proj_new, proj_old, first_old, second_old):
    flip = lambda a: jnp.transpose(a, (1, 0, 2))
    shape = jax.ShapeDtypeStruct((3, 16, C), F32)
    dma = pltpu.SemaphoreType.DMA
    low, turned_first, turned_second = pl.pallas_call(
        kernel,
        out_shape=(shape,) * 3,
        in_specs=[pl.BlockSpec(memory_space=pl.ANY)] * 9,
        out_specs=(pl.BlockSpec(memory_space=pl.ANY),) * 3,
        scratch_shapes=[
            pltpu.VMEM((SH, D), BF16),
            pltpu.VMEM((TOK, D), BF16),
            pltpu.VMEM((TOK, 3 * RANK), BF16),
            pltpu.VMEM((D, RANK), BF16),
            pltpu.VMEM((TOK, C), BF16),
            pltpu.VMEM((TOK, C), BF16),
            pltpu.VMEM((C, D), BF16),
            pltpu.VMEM((3, D, RANK), BF16),
            pltpu.VMEM((3, 16, C), F32),
            pltpu.VMEM((3, 16, C), F32),
            pltpu.VMEM((TOK, C), F32),
            pltpu.VMEM((TOK, C), F32),
            pltpu.VMEM((TOK, C), BF16),
            pltpu.VMEM((TOK, CH), F32),
            pltpu.VMEM((TOK, CH), BF16),
            pltpu.VMEM((TOK, CH), BF16),
            pltpu.VMEM((27, RANK, 128), F32),
            pltpu.VMEM((RANK, RANK), F32),
            pltpu.VMEM((2, RANK, RANK), F32),
            pltpu.VMEM((2, RANK, RANK), F32),
            pltpu.VMEM((15, 72, 128), BF16),
            pltpu.VMEM((16, 72, 128), BF16),
            pltpu.VMEM((16, 72, 128), BF16),
            pltpu.VMEM((15, 72, 128), BF16),
            pltpu.VMEM((27, 32, 128), F32),
            pltpu.VMEM((9, 16, C), F32),
            pltpu.VMEM((7, ROWS, 128), BF16),
            pltpu.VMEM((7, ROWS, 128), BF16),
            pltpu.VMEM((XROWS, 128), BF16),
            pltpu.VMEM((XROWS, 128), BF16),
            dma((10,)), dma((3,)), dma((3, 8)), dma, dma, dma, dma,
            dma, dma((NQ, 7)), dma, dma((NQ,)),
        ],
        compiler_params=pltpu.CompilerParams(
            collective_id=0, has_side_effects=True, vmem_limit_bytes=63 * 1024 * 1024
        ),
    )(
        inputs, out_grad, gate_pre, up_pre, w_down, flip(proj_new), flip(proj_old),
        flip(first_old), flip(second_old),
    )
    first = 0.9 * turned_first + 0.1 * low
    second = 0.999 * turned_second + 0.001 * low * low
    return flip(first), flip(second)


def solution(mesh):
    placed = (
        P(("dp", "tensor"), None),
        P(("dp", "tensor"), None),
        P("dp", "tensor"),
        P("dp", "tensor"),
        P("tensor", None),
        P(),
        P("tensor", None, None),
        P("dp", None, "tensor"),
        P("dp", None, "tensor"),
    )
    return jax.shard_map(
        on_device,
        mesh=mesh,
        in_specs=placed,
        out_specs=(P("dp", None, "tensor"), P("dp", None, "tensor")),
        check_vma=False,
    )
```

time: 85.2 us -> 69.5 us (0.82)
  Pallas kernels: 80.8 us -> 66.8 us
  local copies, waits for them, and re-layouts: 3.27 us -> 0 us
  other arithmetic: 0 us -> 1.97 us
    pallas_call x1, Pallas kernels: 80.8 us -> 66.8 us  [on_device(): pl.pallas_call(kernel, out_shape=(shape,) * 3, in_specs=[pl.BlockSpec(mem...]
    unnamed x2 -> x0, local copies, waits for them, and re-layouts: 3.27 us -> none
    transpose x0 -> x1, other arithmetic: none -> 1.97 us  [on_device(): flip = lambda a: jnp.transpose(a, (1, 0, 2))]
where the time goes in v2:
time: 69.5 us; the launch traced here: 69.4 us
  Pallas kernels  66.8 us (96%)
  other arithmetic  1.97 us (3%)
    pallas_call x1, Pallas kernels, on_device(): pl.pallas_call(kernel, out_shape=(shape,) * 3, in_specs=[pl.BlockSpec(mem...  66.8 us
    transpose x1, other arithmetic, on_device(): flip = lambda a: jnp.transpose(a, (1, 0, 2))  1.97 us

profile of v2, /device:TPU:6, one launch (start us, length us, event | category | flops | bytes accessed | tf_op | source)
XLA Modules:
  0.0 69.4 jit_solution(6903596894844128736)
XLA Ops:
  0.6 66.8 %shard_map.104 = (f32[3,16,1152]{2,1,0:T(8,128)}, f32[3,16,1152]{2,1,0:T(8,128)}, f32[3,16,1152]{2,1,0:T(8,128)}) custom-call(bf16[32,2304]{1,0:T(8,128)(2,1)} %inp_h.1, bf16[32,2304]{1,0:T(8,128)(2,1)} %og_h.1, bf16[512,1152]{1,0:T(8,128)(2,1)} %gate_h.1, bf16[512,1152]{1,0:T(8,128)(2,1)} %up_h.1, bf16[1152,2304]{1,0:T(8,128)(2,1)} %w_h.1, ...), custom_call_target="tpu_custom_call" | custom-call | tf_op jit(solution)/shard_map/pallas_call | solution.py:475
  67.4 2.0 %fusion.1 = (f32[16,3,1152]{2,0,1:T(8,128)}, f32[16,3,1152]{2,0,1:T(8,128)}) fusion(f32[3,16,1152]{2,1,0:T(8,128)} %get-tuple-element.6, f32[3,16,1152]{2,1,0:T(8,128)} %get-tuple-element.7, f32[3,16,1152]{2,1,0:T(8,128)} %get-tuple-element.5), kind=kLoop, calls=%fused_computation.2 | loop fusion | flops 387072 | bytes 1105920 | tf_op jit(solution)/shard_map/transpose | solution.py:472

commit v3 on v2

--- a/solution.py
+++ b/solution.py
@@ -18,10 +18,15 @@
 QT0 = (0, 5, 9, 15, 21)
 QN = (5, 4, 6, 6, 6)
 NQ = 5
-ROWS = 27 * 32 + 8 * NQ
-XROWS = 27 * 16 + 8 * NQ
+XF = (False, False, True, False, False)
+CR = tuple(16 if f else 32 for f in XF)
+XR = tuple(128 if f else 16 for f in XF)
+OFF = tuple(sum(QN[i] * CR[i] + 8 for i in range(q)) for q in range(NQ + 1))
+XOFF = tuple(sum(QN[i] * XR[i] + 8 for i in range(q)) for q in range(NQ + 1))
+ROWS = OFF[NQ]
+XROWS = XOFF[NQ]
 BACK = (0, 2, 1, 3, 5, 4, 6)
-TOP = 32768.0
+TOP = 181.0
 MESH = pl.DeviceIdType.MESH
 
 
@@ -35,12 +40,13 @@
     u = x * (TOP / top.astype(F32))[0:1][None]
     u2 = u * u
     u4 = u2 * u2
-    return ((u4 * u2) * (u * jnp.abs(u))).astype(BF16).reshape(n * rows, 128)
+    u8 = u4 * u4
+    return ((u8 * u4) * (u2 * (u * jnp.abs(u)))).astype(BF16).reshape(n * rows, 128)
 
 
 def value(v, scale, n):
     v = v.astype(F32)
-    r = jnp.exp2(jnp.log2(jnp.abs(v)) * 0.125)
+    r = jnp.exp2(jnp.log2(jnp.abs(v)) * 0.0625)
     return (jnp.where(v < 0.0, -r, r) * (scale * (1.0 / TOP))).reshape(n, -1, 128)
 
 
@@ -72,9 +78,9 @@
 def kernel(
     inp_h, og_h, gate_h, up_h, w_h, pn_h, po_h, fo_h, so_h,
     low_h, tf_h, ts_h,
-    inp, Y, Pb, old, gate, up, w, pn, fo, so, V, U, G, H, GG, UG, L, R, M, T, MS, MR, TS, TB, FIN, OUT,
+    inp, Y, Pb, po, gate, up, w, pn, fo, so, V, U, G, H, GG, UG, L, R, M, T, MS, MR, TS, TB, FIN, OUT, RA, RB, RC, RD,
     rsend, rrecv, xsend, xrecv,
-    ld, gs, gr, ms, mr, ts, tr, rs, rr, xs, xr,
+    ld, gs, gr, ms, mr, ts, tr, rs, rr, xs, xr, ras, rar, rcs, rcr,
 ):
     d = lax.axis_index("dp")
     t = lax.axis_index("tensor")
@@ -112,29 +118,32 @@
     loads = [
         loc(og_h, Y.at[own], 0),
         loc(inp_h, inp, 1),
-        loc(pn_h, pn, 2),
-        loc(po_h.at[kd], old.at[pl.ds(pl.multiple_of(t * SLAB, 16), SLAB)], 3),
+        loc(pn_h.at[2], pn.at[2], 2),
+        loc(po_h.at[kd], po, 3),
         loc(gate_h, gate, 4),
         loc(up_h, up, 5),
         loc(w_h, w, 6),
         loc(fo_h, fo, 7),
         loc(so_h, so, 8),
+        loc(pn_h.at[0], pn.at[0], 10),
+        loc(pn_h.at[1], pn.at[1], 11),
     ]
-    for i in (1, 0, 2, 7, 8, 3):
+    for i in (0, 2, 1, 9, 10, 7, 8, 3):
         loads[i].start()
 
     bar = pltpu.get_barrier_semaphore()
     lane = (xp, yp, ym, tid(xl, y2), tid(xo, yn), tid(xo, yb), tid(xo, y2))
-    for peer in (sib,) + lane:
-        pl.semaphore_signal(bar, inc=1, device_id={"tensor": peer}, device_id_type=MESH)
 
     @pl.loop(1, 16)
     def _(j):
         pl.semaphore_signal(
+            bar, inc=1, device_id={"tensor": lax.rem(t + j, 16)}, device_id_type=MESH
+        )
+        pl.semaphore_signal(
             bar, inc=1, device_id={"dp": lax.rem(d + j, 16)}, device_id_type=MESH
         )
 
-    pay = ((Pb, SH, SH), (Y, SH, SH), (old, SLAB, 16))
+    pay = ((Pb, SH, SH), (Y, SH, SH))
 
     def gcopy(p, slot, target, i):
         buf, rows, mult = pay[p]
@@ -156,15 +165,17 @@
         pltpu.make_async_copy(part, part, sem).wait()
 
     def project():
-        for a in loads[:3]:
-            a.wait()
-        for i in (4, 5, 6):
-            loads[i].start()
-        for k in range(3):
+        for a in (0, 2, 1, 9, 10):
+            loads[a].wait()
+            if a in (0, 1):
+                continue
+            k = (2, 0, 1)[(2, 9, 10).index(a)]
             lhs = inp[...] if k < 2 else Y[own, :]
             Pb[own, k * RANK : (k + 1) * RANK] = jnp.dot(
                 lhs, pn[k], preferred_element_type=F32
             ).astype(BF16)
+        for i in (4, 5, 6):
+            loads[i].start()
 
     def gown(p, n):
         for j in range(n):
@@ -174,21 +185,53 @@
     def gmirror(p, js):
         for j in js:
             gwait(p, j)
-            gsend(p, lane[j], sib, 7)
+            gsend(p, lane[j], sib, 7 if j in (1, 2, 3) else 8)
 
     def gpair(p):
         gwait(p, 0)
         gsend(p, xp, yp, 5)
         gsend(p, xp, ym, 4)
-        gsend(p, xp, sib, 7)
+        gsend(p, xp, sib, 8)
 
     def gfar(p):
         gwait(p, 3)
         gsend(p, lane[3], xp, 6)
         gsend(p, lane[3], sib, 7)
 
-    def g3(p):
-        shards(p, 8, gr.at[p, 7])
+    def g3(p, side):
+        shards(p, 4, gr.at[p, 7 + side])
+
+    def rpart():
+        loads[3].wait()
+        slab = pl.ds(pl.multiple_of(t * SLAB, 16), SLAB)
+        R[...] = lax.dot_general(
+            pn[kd, slab, :], po[...], (((0,), (0,)), ((), ())), preferred_element_type=F32
+        )
+        for j in range(16):
+            rows = slice(16 * j, 16 * j + 16)
+            enc(jnp.stack([R[rows, 0:128], R[rows, 128:256]]), RA.at[j])
+
+    def spread(src, dst, ssem, rsem):
+        @pl.loop(1, 16)
+        def _(i):
+            j = lax.rem(t + i, 16)
+            pltpu.make_async_remote_copy(
+                src_ref=src(j), dst_ref=dst, send_sem=ssem, recv_sem=rsem,
+                device_id={"tensor": j}, device_id_type=MESH,
+            ).start()
+
+        pltpu.make_async_copy(src(t), dst, rsem).start()
+
+    def rsend1():
+        spread(lambda j: RA.at[j], RB.at[t], ras, rar)
+
+    def rsum():
+        pltpu.make_async_copy(RB, RB, rar).wait()
+        x = dec(RB.at[0], 2, 16)
+        for j in range(1, 16):
+            x = x + dec(RB.at[j], 2, 16)
+        enc(x, RC)
+        spread(lambda j: RC, RD.at[t], rcs, rcr)
 
     def mrem(o):
         return pltpu.make_async_remote_copy(
@@ -227,9 +270,7 @@
         )
 
     def turn():
-        R[...] = lax.dot_general(
-            pn[kd], old[...], (((0,), (0,)), ((), ())), preferred_element_type=F32
-        )
+        pltpu.make_async_copy(RD, RD, rcr).wait()
 
         @pl.when(d < 15)
         def _():
@@ -242,6 +283,10 @@
                     M[m, rows, 0:128] = x[0]
                     M[m, rows, 128:256] = x[1]
 
+            for j in range(16):
+                x = dec(RD.at[j], 2, 16)
+                R[16 * j : 16 * j + 16, 0:128] = x[0]
+                R[16 * j : 16 * j + 16, 128:256] = x[1]
             rot = R[...]
             for m in range(2):
                 T[m] = jnp.dot(
@@ -249,22 +294,29 @@
                     precision=lax.Precision.HIGHEST, preferred_element_type=F32,
                 )
 
-            @pl.loop(0, 16)
-            def _(j):
+    def tsend(lo, hi):
+        @pl.when(d < 15)
+        def _():
+            @pl.loop(lo, hi)
+            def _(i):
+                j = lax.rem(d + i, 16)
                 rows = pl.ds(pl.multiple_of(j * 16, 16), 16)
                 pair = [jnp.stack([T[m, rows, 0:128], T[m, rows, 128:256]]) for m in range(2)]
                 enc2(*pair, TS.at[j])
 
-                @pl.when(j != d)
+                @pl.when(i > 0)
                 def _():
                     trem(j).start()
 
-                @pl.when(j == d)
+                @pl.when(i == 0)
                 def _():
                     pltpu.make_async_copy(TS.at[j], TB.at[d], tr).start()
 
-    def span(q, rows=32):
-        return pl.ds(QT0[q] * rows + 8 * q, QN[q] * rows + 8)
+    def span(q):
+        return pl.ds(OFF[q], OFF[q + 1] - OFF[q])
+
+    def xspan(q):
+        return pl.ds(XOFF[q], XOFF[q + 1] - XOFF[q])
 
     def rcopy(q, i):
         sp = span(q)
@@ -274,7 +326,10 @@
         )
 
     def mine(q, zdest):
-        return L[pl.ds(QT0[q], QN[q]), pl.ds(pl.multiple_of(zdest * 32, 32), 32), :]
+        tiles = pl.ds(QT0[q], QN[q])
+        if XF[q]:
+            return L[tiles, zdest, xh]
+        return L[tiles, zdest].reshape(QN[q], 32, 128)
 
     def rnd(q, r):
         n = QN[q]
@@ -285,32 +340,32 @@
             x = mine(q, lax.rem(z + 8 + far, 8))
             if r > 0:
                 rcopy(q, i - 1).wait_recv()
-                x = x + dec(rrecv.at[i - 1, tiles], n, 32)
+                x = x + dec(rrecv.at[i - 1, tiles], n, CR[q])
             enc(x, rsend.at[i, tiles])
             rcopy(q, i).start()
 
     def xcopy(q):
-        sp = span(q, 16)
+        sp = xspan(q)
         return pltpu.make_async_remote_copy(
             src_ref=xsend.at[sp], dst_ref=xrecv.at[sp], send_sem=xs, recv_sem=xr.at[q],
             device_id={"dp": dx}, device_id_type=MESH,
         )
 
-    def fin(q):
+    def xout(q):
         n = QN[q]
-        tiles = span(q)
-        dst = pl.ds(QT0[q], n)
-        rcopy(q, 3).wait_recv()
-        rcopy(q, 6).wait_recv()
-        FIN[dst] = mine(q, z) + dec(rrecv.at[3, tiles], n, 32) + dec(rrecv.at[6, tiles], n, 32)
-        enc(FIN[dst, pl.ds(pl.multiple_of((1 - xh) * 16, 16), 16), :], xsend.at[span(q, 16)])
+        x = L[pl.ds(QT0[q], n), :, 1 - xh]
+        enc(x.reshape(n, 128, 128), xsend.at[xspan(q)])
         xcopy(q).start()
 
-    def last(q):
+    def xin(q):
         n = QN[q]
-        dst = pl.ds(QT0[q], n)
+        tiles = pl.ds(QT0[q], n)
         xcopy(q).wait_recv()
-        low = FIN[dst, pl.ds(pl.multiple_of(xh * 16, 16), 16), :] + dec(xrecv.at[span(q, 16)], n, 16)
+        x = dec(xrecv.at[xspan(q)], n, 128)
+        L[tiles, :, xh] = L[tiles, :, xh] + x.reshape(n, 8, 16, 128)
+
+    def emit(q, low):
+        n = QN[q]
         for i in range(n):
             g = QT0[q] + i
             k, ct = (2, g) if g < 9 else ((g - 9) % 6 // 3, (g - 9) // 6 * 3 + (g - 9) % 3)
@@ -320,6 +375,30 @@
         else:
             part = (pl.ds(0, 2), slice(None), pl.ds((q - 2) * CH, CH))
         pltpu.make_async_copy(OUT.at[part], low_h.at[part], ld.at[9]).start()
+
+    def fin(q):
+        n = QN[q]
+        tiles = span(q)
+        dst = pl.ds(QT0[q], n)
+        rcopy(q, 3).wait_recv()
+        rcopy(q, 6).wait_recv()
+        x = mine(q, z) + dec(rrecv.at[3, tiles], n, CR[q]) + dec(rrecv.at[6, tiles], n, CR[q])
+        if XF[q]:
+            emit(q, x)
+            return
+        FIN[dst] = x
+        enc(FIN[dst, pl.ds(pl.multiple_of((1 - xh) * 16, 16), 16), :], xsend.at[xspan(q)])
+        xcopy(q).start()
+
+    def last(q):
+        n = QN[q]
+        dst = pl.ds(QT0[q], n)
+        xcopy(q).wait_recv()
+        emit(
+            q,
+            FIN[dst, pl.ds(pl.multiple_of(xh * 16, 16), 16), :]
+            + dec(xrecv.at[xspan(q)], n, 16),
+        )
 
     def back():
         pltpu.make_async_copy(TB, TB, tr).wait()
@@ -333,11 +412,12 @@
         loc(OUT.at[pl.ds(6, 3)], ts_h, 9).start()
 
     project()
-    pl.semaphore_wait(bar, 23)
+    pl.semaphore_wait(bar, 30)
     gown(0, 7)
     gown(1, 4)
     menc()
     msend(xh)
+    rpart()
     loads[4].wait()
     loads[5].wait()
 
@@ -366,31 +446,40 @@
                 preferred_element_type=F32,
             )
             for i in range(3):
-                L[3 * j + i] = r[:, i * 128 : (i + 1) * 128]
-
-    def chunk(j):
+                L[3 * j + i] = r[:, i * 128 : (i + 1) * 128].reshape(8, 2, 16, 128)
+
+    def chunk(j, side):
         cols = slice(j * CH, (j + 1) * CH)
+        row0 = (xl if side == 0 else xo) * 256
+        part = pl.ds(pl.multiple_of(row0, 256), 256)
         H[...] = lax.dot_general(
-            Y[...], w[cols, :], (((1,), (1,)), ((), ())), preferred_element_type=F32
-        )
-
-        @pl.loop(0, 16)
+            Y[part, :], w[cols, :], (((1,), (1,)), ((), ())), preferred_element_type=F32
+        )
+
+        @pl.loop(0, 8)
         def _(i):
             rows = pl.ds(pl.multiple_of(i * 32, 32), 32)
+            from_ = pl.ds(pl.multiple_of(row0 + i * 32, 32), 32)
             h = H[rows, :]
-            GG[rows, :] = (h * U[rows, cols]).astype(BF16)
-            UG[rows, :] = (h * V[rows, cols]).astype(BF16)
+            GG[rows, :] = (h * U[from_, cols]).astype(BF16)
+            UG[rows, :] = (h * V[from_, cols]).astype(BF16)
 
         for k, ref in enumerate((GG, UG)):
             r = lax.dot_general(
-                Pb[:, k * RANK : (k + 1) * RANK], ref[...], contract, preferred_element_type=F32
+                Pb[part, k * RANK : (k + 1) * RANK], ref[...], contract,
+                preferred_element_type=F32,
             )
             for i in range(3):
-                L[9 + 6 * j + 3 * k + i] = r[:, i * 128 : (i + 1) * 128]
+                tile = r[:, i * 128 : (i + 1) * 128].reshape(8, 2, 16, 128)
+                g = 9 + 6 * j + 3 * k + i
+                L[g] = tile if side == 0 else L[g] + tile
 
     def gdrain():
-        for p in range(3):
+        for p in range(2):
             shards(p, 15, gs.at[p])
+        part = RA.at[pl.ds(0, 15)]
+        pltpu.make_async_copy(part, part, ras).wait()
+        pltpu.make_async_copy(part, part, rcs).wait()
 
     def mdrain():
         @pl.when(d < 15)
@@ -411,59 +500,64 @@
 
     act(0, 32)
     gmirror(0, range(7))
-    gpair(1)
-    msend(1 - xh)
-    g3(0)
+    g3(0, 0)
+    g3(0, 1)
     lowd()
     rnd(0, 0)
     rnd(1, 0)
+    gpair(1)
+    rsend1()
+    gmirror(1, (1, 2))
     gfar(1)
-    loads[3].wait()
-    gown(2, 4)
-    gmirror(1, (1, 2))
+    msend(1 - xh)
     rnd(0, 1)
     rnd(1, 1)
+    loads[6].wait()
+    g3(1, 0)
+    chunk(0, 0)
     gmirror(1, (4, 5))
-    gpair(2)
+    chunk(1, 0)
+    rsum()
     gmirror(1, (6,))
-    loads[6].wait()
+    chunk(2, 0)
+    g3(1, 1)
+    chunk(0, 1)
+    xout(2)
     rnd(0, 2)
-    g3(1)
-    chunk(0)
+    rnd(1, 2)
+    chunk(1, 1)
+    rnd(3, 0)
+    chunk(2, 1)
+    rnd(4, 0)
+    rnd(0, 3)
+    rnd(1, 3)
+    turn()
+    tsend(0, 4)
+    rnd(3, 1)
+    xin(2)
     rnd(2, 0)
-    rnd(1, 2)
-    gfar(2)
-    gmirror(2, (1, 2, 4, 5))
-    rnd(0, 3)
-    chunk(1)
-    rnd(3, 0)
+    rnd(4, 1)
+    tsend(4, 8)
+    rnd(3, 2)
     rnd(2, 1)
-    rnd(1, 3)
-    gmirror(2, (6,))
-    g3(2)
-    turn()
+    rnd(4, 2)
+    tsend(8, 12)
     fin(0)
-    rnd(3, 1)
+    fin(1)
+    rnd(3, 3)
     rnd(2, 2)
-    chunk(2)
-    rnd(4, 0)
-    rnd(3, 2)
+    tsend(12, 16)
+    rnd(4, 3)
+    fin(3)
     rnd(2, 3)
-    fin(1)
-    rnd(4, 1)
+    gdrain()
+    mdrain()
     last(0)
     last(1)
-    rnd(3, 3)
-    fin(2)
-    rnd(4, 2)
-    fin(3)
-    rnd(4, 3)
-    last(2)
-    gdrain()
-    mdrain()
-    back()
     fin(4)
     last(3)
+    fin(2)
+    back()
     last(4)
     rdrain()
 
@@ -481,7 +575,7 @@
             pltpu.VMEM((SH, D), BF16),
             pltpu.VMEM((TOK, D), BF16),
             pltpu.VMEM((TOK, 3 * RANK), BF16),
-            pltpu.VMEM((D, RANK), BF16),
+            pltpu.VMEM((SLAB, RANK), BF16),
             pltpu.VMEM((TOK, C), BF16),
             pltpu.VMEM((TOK, C), BF16),
             pltpu.VMEM((C, D), BF16),
@@ -491,10 +585,10 @@
             pltpu.VMEM((TOK, C), F32),
             pltpu.VMEM((TOK, C), F32),
             pltpu.VMEM((TOK, C), BF16),
-            pltpu.VMEM((TOK, CH), F32),
-            pltpu.VMEM((TOK, CH), BF16),
-            pltpu.VMEM((TOK, CH), BF16),
-            pltpu.VMEM((27, RANK, 128), F32),
+            pltpu.VMEM((256, CH), F32),
+            pltpu.VMEM((256, CH), BF16),
+            pltpu.VMEM((256, CH), BF16),
+            pltpu.VMEM((27, 8, 2, 16, 128), F32),
             pltpu.VMEM((RANK, RANK), F32),
             pltpu.VMEM((2, RANK, RANK), F32),
             pltpu.VMEM((2, RANK, RANK), F32),
@@ -504,12 +598,16 @@
             pltpu.VMEM((15, 72, 128), BF16),
             pltpu.VMEM((27, 32, 128), F32),
             pltpu.VMEM((9, 16, C), F32),
+            pltpu.VMEM((16, 40, 128), BF16),
+            pltpu.VMEM((16, 40, 128), BF16),
+            pltpu.VMEM((40, 128), BF16),
+            pltpu.VMEM((16, 40, 128), BF16),
             pltpu.VMEM((7, ROWS, 128), BF16),
             pltpu.VMEM((7, ROWS, 128), BF16),
             pltpu.VMEM((XROWS, 128), BF16),
             pltpu.VMEM((XROWS, 128), BF16),
-            dma((10,)), dma((3,)), dma((3, 8)), dma, dma, dma, dma,
-            dma, dma((NQ, 7)), dma, dma((NQ,)),
+            dma((12,)), dma((2,)), dma((2, 9)), dma, dma, dma, dma,
+            dma, dma((NQ, 7)), dma, dma((NQ,)), dma, dma, dma, dma,
         ],
         compiler_params=pltpu.CompilerParams(
             collective_id=0, has_side_effects=True, vmem_limit_bytes=63 * 1024 * 1024

time: 69.5 us -> 63.7 us (0.917)
  the two profiles are of different devices: /device:TPU:6 before, /device:TPU:1 now
where the time goes in v3:
time: 63.7 us; the launch traced here: 63.6 us
  Pallas kernels  61 us (96%)
  other arithmetic  1.97 us (3%)
  between operations  0.64 us (1%)
    pallas_call x1, Pallas kernels, on_device(): pl.pallas_call(kernel, out_shape=(shape,) * 3, in_specs=[pl.BlockSpec(mem...  61 us
    transpose x1, other arithmetic, on_device(): flip = lambda a: jnp.transpose(a, (1, 0, 2))  1.97 us

profile of v3, /device:TPU:1, one launch (start us, length us, event | category | flops | bytes accessed | tf_op | source)
XLA Modules:
  0.0 63.6 jit_solution(5816893740567399032)
XLA Ops:
  0.6 61.0 %shard_map.104 = (f32[3,16,1152]{2,1,0:T(8,128)}, f32[3,16,1152]{2,1,0:T(8,128)}, f32[3,16,1152]{2,1,0:T(8,128)}) custom-call(bf16[32,2304]{1,0:T(8,128)(2,1)} %inp_h.1, bf16[32,2304]{1,0:T(8,128)(2,1)} %og_h.1, bf16[512,1152]{1,0:T(8,128)(2,1)} %gate_h.1, bf16[512,1152]{1,0:T(8,128)(2,1)} %up_h.1, bf16[1152,2304]{1,0:T(8,128)(2,1)} %w_h.1, ...), custom_call_target="tpu_custom_call" | custom-call | tf_op jit(solution)/shard_map/pallas_call | solution.py:569
  61.6 2.0 %fusion.1 = (f32[16,3,1152]{2,0,1:T(8,128)}, f32[16,3,1152]{2,0,1:T(8,128)}) fusion(f32[3,16,1152]{2,1,0:T(8,128)} %get-tuple-element.6, f32[3,16,1152]{2,1,0:T(8,128)} %get-tuple-element.7, f32[3,16,1152]{2,1,0:T(8,128)} %get-tuple-element.5), kind=kLoop, calls=%fused_computation.2 | loop fusion | flops 387072 | bytes 1105920 | tf_op jit(solution)/shard_map/transpose | solution.py:566

commit v4 on v3

--- a/solution.py
+++ b/solution.py
@@ -108,6 +108,7 @@
     zshort = jnp.where(c == 0, zb, zn)
     dlong = zlong * 2 + xh
     dshort = zshort * 2 + xh
+    dfar = lax.rem(z + 8 + 2 * (1 - 2 * c), 8) * 2 + xh
     dx = d + 1 - 2 * xh
     step = 1 - 2 * c
 
@@ -322,7 +323,7 @@
         sp = span(q)
         return pltpu.make_async_remote_copy(
             src_ref=rsend.at[i, sp], dst_ref=rrecv.at[i, sp], send_sem=rs, recv_sem=rr.at[q, i],
-            device_id={"dp": dlong if i < 4 else dshort}, device_id_type=MESH,
+            device_id={"dp": dlong if i < 3 else dshort if i < 6 else dfar}, device_id_type=MESH,
         )
 
     def mine(q, zdest):
@@ -334,13 +335,16 @@
     def rnd(q, r):
         n = QN[q]
         tiles = span(q)
-        for i, far in ((r, step * (4 - r)), (4 + r, -step * (3 - r))):
-            if i == 7:
+        for i, far in ((6, 4), (r, step * (3 - r)), (3 + r, -step * (3 - r))):
+            if i == 6 and r > 0:
                 continue
             x = mine(q, lax.rem(z + 8 + far, 8))
             if r > 0:
                 rcopy(q, i - 1).wait_recv()
                 x = x + dec(rrecv.at[i - 1, tiles], n, CR[q])
+            if i == 1:
+                rcopy(q, 6).wait_recv()
+                x = x + dec(rrecv.at[6, tiles], n, CR[q])
             enc(x, rsend.at[i, tiles])
             rcopy(q, i).start()
 
@@ -380,9 +384,9 @@
         n = QN[q]
         tiles = span(q)
         dst = pl.ds(QT0[q], n)
-        rcopy(q, 3).wait_recv()
-        rcopy(q, 6).wait_recv()
-        x = mine(q, z) + dec(rrecv.at[3, tiles], n, CR[q]) + dec(rrecv.at[6, tiles], n, CR[q])
+        rcopy(q, 2).wait_recv()
+        rcopy(q, 5).wait_recv()
+        x = mine(q, z) + dec(rrecv.at[2, tiles], n, CR[q]) + dec(rrecv.at[5, tiles], n, CR[q])
         if XF[q]:
             emit(q, x)
             return
@@ -529,8 +533,6 @@
     rnd(3, 0)
     chunk(2, 1)
     rnd(4, 0)
-    rnd(0, 3)
-    rnd(1, 3)
     turn()
     tsend(0, 4)
     rnd(3, 1)
@@ -544,12 +546,9 @@
     tsend(8, 12)
     fin(0)
     fin(1)
-    rnd(3, 3)
     rnd(2, 2)
     tsend(12, 16)
-    rnd(4, 3)
     fin(3)
-    rnd(2, 3)
     gdrain()
     mdrain()
     last(0)

time: 63.7 us -> 62 us (0.973)
  the two profiles are of different devices: /device:TPU:1 before, /device:TPU:6 now
where the time goes in v4:
time: 62 us; the launch traced here: 61.9 us
  Pallas kernels  59.3 us (96%)
  other arithmetic  1.97 us (3%)
  between operations  0.64 us (1%)
    pallas_call x1, Pallas kernels, on_device(): pl.pallas_call(kernel, out_shape=(shape,) * 3, in_specs=[pl.BlockSpec(mem...  59.3 us
    transpose x1, other arithmetic, on_device(): flip = lambda a: jnp.transpose(a, (1, 0, 2))  1.97 us

profile of v4, /device:TPU:6, one launch (start us, length us, event | category | flops | bytes accessed | tf_op | source)
XLA Modules:
  0.0 61.9 jit_solution(13378590314191145585)
XLA Ops:
  0.6 59.3 %shard_map.104 = (f32[3,16,1152]{2,1,0:T(8,128)}, f32[3,16,1152]{2,1,0:T(8,128)}, f32[3,16,1152]{2,1,0:T(8,128)}) custom-call(bf16[32,2304]{1,0:T(8,128)(2,1)} %inp_h.1, bf16[32,2304]{1,0:T(8,128)(2,1)} %og_h.1, bf16[512,1152]{1,0:T(8,128)(2,1)} %gate_h.1, bf16[512,1152]{1,0:T(8,128)(2,1)} %up_h.1, bf16[1152,2304]{1,0:T(8,128)(2,1)} %w_h.1, ...), custom_call_target="tpu_custom_call" | custom-call | tf_op jit(solution)/shard_map/pallas_call | solution.py:568
  60.0 2.0 %fusion.1 = (f32[16,3,1152]{2,0,1:T(8,128)}, f32[16,3,1152]{2,0,1:T(8,128)}) fusion(f32[3,16,1152]{2,1,0:T(8,128)} %get-tuple-element.6, f32[3,16,1152]{2,1,0:T(8,128)} %get-tuple-element.7, f32[3,16,1152]{2,1,0:T(8,128)} %get-tuple-element.5), kind=kLoop, calls=%fused_computation.2 | loop fusion | flops 387072 | bytes 1105920 | tf_op jit(solution)/shard_map/transpose | solution.py:565

commit v5 on v4

--- a/solution.py
+++ b/solution.py
@@ -546,17 +546,17 @@
     tsend(8, 12)
     fin(0)
     fin(1)
+    tsend(12, 16)
     rnd(2, 2)
-    tsend(12, 16)
     fin(3)
-    gdrain()
-    mdrain()
+    fin(4)
     last(0)
     last(1)
-    fin(4)
     last(3)
     fin(2)
     back()
+    gdrain()
+    mdrain()
     last(4)
     rdrain()
 

time: 62 us -> 61.4 us (level)
  Pallas kernels: 59.3 us -> 58.6 us
    pallas_call x1, Pallas kernels: 59.3 us -> 58.6 us  [on_device(): pl.pallas_call(kernel, out_shape=(shape,) * 3, in_specs=[pl.BlockSpec(mem...]
where the time goes in v5:
time: 61.4 us; the launch traced here: 61.2 us
  Pallas kernels  58.6 us (95%)
  other arithmetic  1.97 us (3%)
  between operations  0.64 us (1%)
    pallas_call x1, Pallas kernels, on_device(): pl.pallas_call(kernel, out_shape=(shape,) * 3, in_specs=[pl.BlockSpec(mem...  58.6 us
    transpose x1, other arithmetic, on_device(): flip = lambda a: jnp.transpose(a, (1, 0, 2))  1.97 us

profile of v5, /device:TPU:6, one launch (start us, length us, event | category | flops | bytes accessed | tf_op | source)
XLA Modules:
  0.0 61.2 jit_solution(2315055274674027112)
XLA Ops:
  0.6 58.6 %shard_map.104 = (f32[3,16,1152]{2,1,0:T(8,128)}, f32[3,16,1152]{2,1,0:T(8,128)}, f32[3,16,1152]{2,1,0:T(8,128)}) custom-call(bf16[32,2304]{1,0:T(8,128)(2,1)} %inp_h.1, bf16[32,2304]{1,0:T(8,128)(2,1)} %og_h.1, bf16[512,1152]{1,0:T(8,128)(2,1)} %gate_h.1, bf16[512,1152]{1,0:T(8,128)(2,1)} %up_h.1, bf16[1152,2304]{1,0:T(8,128)(2,1)} %w_h.1, ...), custom_call_target="tpu_custom_call" | custom-call | tf_op jit(solution)/shard_map/pallas_call | solution.py:568
  59.2 2.0 %fusion.1 = (f32[16,3,1152]{2,0,1:T(8,128)}, f32[16,3,1152]{2,0,1:T(8,128)}) fusion(f32[3,16,1152]{2,1,0:T(8,128)} %get-tuple-element.6, f32[3,16,1152]{2,1,0:T(8,128)} %get-tuple-element.7, f32[3,16,1152]{2,1,0:T(8,128)} %get-tuple-element.5), kind=kLoop, calls=%fused_computation.2 | loop fusion | flops 387072 | bytes 1105920 | tf_op jit(solution)/shard_map/transpose | solution.py:565
